TPU v7x, 128 devices: a whole 4x4x4 slice. The times are simulated.
128 devices in a mesh: blk: 32 (over x, z, core), tok: 4 (over y).
Axes of the slice: x: 4, y: 4, z: 4, core: 2. Of those that a mesh axis runs over, the one named last changes fastest.
Arguments:
- stream: bfloat16 [16384, 1664], P(('tok', 'blk'))
- queries: bfloat16 [16384, 1664], P(('tok', 'blk'))
- key_cache: bfloat16 [16384, 1664], P(('tok', 'blk'))
- value_cache: bfloat16 [16384, 1664], P(('tok', 'blk')), may hold values from -6 to 6
- segments: int32 [16384], P('tok'), may hold values from 63 to 16383, as said below
- stale_rows: int32 [1536], P(('tok', 'blk')), may hold values from 0 to 16383, as said below
- owners: int32 [4096], P(('tok', 'blk')), may hold values from 0 to 3, as said below
- attn_gain: float32 [1664], replicated, may hold values from 0.1 to 1.9
- w_key: bfloat16 [1664, 1664], replicated, may hold values from -0.15625 to 0.15625
- key_bias: float32 [1664], replicated, may hold values from -3 to 3
- mlp_gain: float32 [1664], replicated, may hold values from 0.1 to 1.9
- w_fc: bfloat16 [1664, 8192], P(None, 'blk'), may hold values from -0.15625 to 0.15625
- b_fc: float32 [8192], P('blk'), may hold values from -3 to 3
- w_proj: bfloat16 [8192, 1664], P('blk'), may hold values from -0.125 to 0.125
- b_proj: float32 [1664], replicated, may hold values from -3 to 3
- merge_gain: float32 [1664], replicated, may hold values from 0.1 to 1.9
- w_merge: bfloat16 [1664, 1664], replicated, may hold values from -0.15625 to 0.15625
- b_merge: float32 [1664], replicated, may hold values from -3 to 3
Outputs:
- refreshed_keys: bfloat16 [16384, 1664], P(('tok', 'blk'))
- delivered: bfloat16 [4, 32, 128, 1664], P('tok', 'blk')
Inputs may be any that keep to these rules, and one draw needn't show every extreme that they name: `segments`: A segment's id is the index of its last row, so ids never fall; each segment has 4 to 128 rows, a multiple of 4, and lies inside one aligned block of 4096 rows; each such block begins with a segment of 64 rows followed by one of exactly 128 rows. `stale_rows`: Distinct; the aligned block of 128 rows of each device holds exactly 12 of them, all inside that block and listed on that device; row 0 and the last row are always listed. `owners`: all merged tokens of one segment (the segment of row 4 m for merged token m) have the same owner.
All inputs are finite; a program needn't handle non-finite values.
Results may differ from a plain program's by a relative error of at most 0.011.
Values may be sent and summed in bfloat16 or wider, within the bound.
No kernel may reach another device: no remote copies, remote signals or barrier semaphores. Data moves between devices by JAX's collectives and lax.ppermute only.
A program may use at most 192 MiB of HBM per device.

v0:
```python
import jax
import jax.numpy as jnp
from jax import lax
from jax.sharding import PartitionSpec as P

HEADS = 16


def passed_along(block, axis, distance):
    devices = range(lax.axis_size(axis))
    route = [(i - distance, i) for i in devices if i - distance in devices]
    return lax.ppermute(block, axis, route)


def layer_norm(values, gain):
    center = values - jnp.mean(values, axis=-1, keepdims=True)
    spread = jnp.mean(center * center, axis=-1, keepdims=True)
    return center * lax.rsqrt(spread + 1e-06) * gain


def body(
    stream,
    queries,
    key_cache,
    value_cache,
    segments,
    stale_rows,
    owners,
    attn_gain,
    w_key,
    key_bias,
    mlp_gain,
    w_fc,
    b_fc,
    w_proj,
    b_proj,
    merge_gain,
    w_merge,
    b_merge,
):
    row_count = stream.shape[0]
    model_width = stream.shape[1]
    head_size = model_width // HEADS
    local_rows = stale_rows % row_count
    held = layer_norm(stream[local_rows].astype(jnp.float32), attn_gain).astype(jnp.bfloat16)
    fresh_keys = (jnp.dot(held, w_key, preferred_element_type=jnp.float32) + key_bias).astype(
        jnp.bfloat16
    )
    refreshed = key_cache.at[local_rows].set(fresh_keys)
    below = passed_along((refreshed, value_cache), "blk", 1)
    above = passed_along((refreshed, value_cache), "blk", -1)
    key_window = jnp.concatenate([below[0], refreshed, above[0]], axis=0).reshape(
        3 * row_count, HEADS, head_size
    )
    value_window = jnp.concatenate([below[1], value_cache, above[1]], axis=0).reshape(
        3 * row_count, HEADS, head_size
    )
    position = lax.axis_index("blk")
    minus_ones = jnp.full((row_count,), -1, jnp.int32)
    seg_padded = jnp.concatenate([minus_ones, segments, minus_ones], axis=0)
    key_seg = lax.dynamic_slice_in_dim(seg_padded, position * row_count, 3 * row_count, 0)
    query_seg = lax.dynamic_slice_in_dim(segments, position * row_count, row_count, 0)
    query_heads = queries.reshape(row_count, HEADS, head_size)
    scores = jnp.einsum(
        "qhd,khd->hqk", query_heads, key_window, preferred_element_type=jnp.float32
    ) * (1.0 / head_size**0.5)
    allowed = (query_seg[:, None] == key_seg[None, :])[None]
    scores = jnp.where(allowed, scores, -jnp.inf)
    top_score = jnp.max(scores, axis=-1, keepdims=True)
    weights = jnp.exp(scores - top_score)
    probs = (weights / jnp.sum(weights, axis=-1, keepdims=True)).astype(jnp.bfloat16)
    attended = jnp.einsum("hqk,khd->qhd", probs, value_window, preferred_element_type=jnp.float32)
    attended = attended.reshape(row_count, model_width).astype(jnp.bfloat16)
    mixed = stream.astype(jnp.float32) + attended.astype(jnp.float32)
    normed = layer_norm(mixed, mlp_gain).astype(jnp.bfloat16)
    group_units = jax.nn.gelu(
        jnp.dot(
            lax.all_gather(normed, "blk", axis=0, tiled=True),
            w_fc,
            preferred_element_type=jnp.float32,
        )
        + b_fc,
        approximate=False,
    ).astype(jnp.bfloat16)
    summed = lax.psum_scatter(
        jnp.dot(group_units, w_proj, preferred_element_type=jnp.float32).astype(jnp.bfloat16),
        "blk",
        scatter_dimension=0,
        tiled=True,
    ).astype(jnp.float32)
    pooled = jnp.mean((mixed + summed).reshape(row_count // 4, 4, model_width), axis=1) + b_proj
    merge_in = layer_norm(pooled, merge_gain).astype(jnp.bfloat16)
    merged = (jnp.dot(merge_in, w_merge, preferred_element_type=jnp.float32) + b_merge).astype(
        jnp.bfloat16
    )
    owner_count = lax.axis_size("tok")
    merged_rows = row_count // 4
    owner_hot = (owners[:, None] == jnp.arange(owner_count, dtype=jnp.int32)[None, :]).astype(
        jnp.int32
    )
    ranking = jnp.sum(jnp.cumsum(owner_hot, axis=0) * owner_hot, axis=-1) - 1
    selector = (
        owners[None, None, :] == jnp.arange(owner_count, dtype=jnp.int32)[:, None, None]
    ) & (ranking[None, None, :] == jnp.arange(merged_rows, dtype=jnp.int32)[None, :, None])
    outgoing = jnp.einsum(
        "osm,md->osd", selector.astype(jnp.bfloat16), merged, preferred_element_type=jnp.float32
    ).astype(jnp.bfloat16)
    arrived = lax.all_to_all(outgoing, "tok", split_axis=0, concat_axis=0, tiled=True)
    delivered = arrived.reshape(1, 1, owner_count * merged_rows, model_width)
    return (refreshed, delivered)


def solution(mesh):
    return jax.shard_map(
        body,
        mesh=mesh,
        in_specs=(
            P(("tok", "blk"), None),
            P(("tok", "blk"), None),
            P(("tok", "blk"), None),
            P(("tok", "blk"), None),
            P("tok"),
            P(("tok", "blk")),
            P(("tok", "blk")),
            P(),
            P(),
            P(),
            P(),
            P(None, "blk"),
            P("blk"),
            P("blk", None),
            P(),
            P(),
            P(),
            P(),
        ),
        out_specs=(P(("tok", "blk"), None), P("tok", "blk", None, None)),
        check_vma=False,
    )
```

profile of v0, /device:TPU:0, one launch (start us, length us, event | category | flops | bytes accessed | tf_op | source)
XLA Modules:
  0.0 274.7 jit_solution(774383592987161788)
XLA Ops:
  7.2 0.0 copy-start
  7.2 0.0 all-gather.2.cloned.1.call-start
  7.3 0.8 compare_select_fusion
  8.1 1.7 gather_fusion
  9.8 0.1 convert_reduce_fusion
  9.9 0.2 fusion.58
  10.1 3.4 %fusion.14 = bf16[12,1664]{1,0:T(8,128)(2,1)S(1)} fusion(bf16[1664,1664]{1,0:T(8,128)(2,1)} %param.26, bf16[12,1664]{1,0:T(8,128)(2,1)S(1)} %gather_fusion, f32[1664]{0:T(1024)} %param.27, f32[1664]{0:T(1024)} %param.25, f32[12]{0:T(128)S(1)} %add_rsqrt_fusion.2, f32[12]{0:T(128)S(1)} %broadcast_multiply_fusion.2), kind=kOutput, calls=%fused_computation.33 | convolution fusion | flops 66593280 | bytes 5631072 | tf_op jit(solution)/shard_map/dot_general | solution.py:46
  13.6 0.9 scatter_fusion
  14.5 0.0 copy-start.2
  14.5 1.3 collective-permute-start.2
  15.9 1.3 collective-permute-start.3
  17.2 5.3 %collective-permute-start = (bf16[128,1664]{1,0:T(8,128)(2,1)S(1)}, bf16[128,1664]{1,0:T(8,128)(2,1)S(1)}, u32[]{:S(2)}, u32[]{:S(2)}) collective-permute-start(bf16[128,1664]{1,0:T(8,128)(2,1)S(1)} %copy-done.5), channel_id=1, source_target_pairs={{0,4},{4,8},{8,12},{12,16},{16,20},{20,24},{24,28},{28,32},{32,36}... | collective-permute-start | bytes 1277960 | tf_op jit(solution)/shard_map/ppermute | solution.py:12
  22.4 1.3 collective-permute-start.1
  23.8 1.0 copy.32
  24.7 0.1 dynamic_slice.6
  24.8 0.1 fusion.82
  24.9 0.1 broadcast_compare_fusion
  25.0 0.0 copy-start.6
  25.1 0.7 copy-done.6
  25.8 1.2 pad_maximum_fusion.1
  27.0 1.5 copy.31
  28.6 1.1 pad_maximum_fusion
  29.7 1.6 copy.30
  31.3 4.4 %fusion.118 = (f32[16,128]{1,0:T(8,128)S(1)}, f32[16,128,384]{1,2,0:T(8,128)}) fusion(pred[128,384]{0,1:T(8,128)(4,1)S(1)} %broadcast_compare_fusion, bf16[384,16,104]{0,2,1:T(8,128)(2,1)} %bitcast.33, bf16[128,16,104]{0,2,1:T(8,128)(2,1)} %bitcast.36), kind=kOutput, calls=%fused_computation.159 | convolution fusion | flops 166723968 | bytes 4907008 | tf_op jit(solution)/shard_map/sub | solution.py:70
  35.7 2.5 fusion.52
  38.2 0.3 copy.34
  38.5 0.0 copy-start.14
  38.6 0.2 fusion.73
  38.7 0.3 multiply_reduce_fusion
  39.0 1.0 multiply_convert_fusion
  40.0 0.0 all-gather.2.cloned.1.call-update
  40.0 0.2 reduce-scatter.2.cloned.1.call-start
  40.2 74.5 %all-gather.2.cloned.1.call-done = bf16[4096,1664]{1,0:T(8,128)(2,1)} async-done(((bf16[128,1664]{1,0:T(8,128)(2,1)}), bf16[4096,1664]{1,0:T(8,128)(2,1)}) %all-gather.2.cloned.1.call-update) | async-done | bytes 13631504 | tf_op jit(solution)/shard_map/all_gather | solution.py:78
  114.7 27.8 %convolution_convert_fusion = bf16[4096,1664]{1,0:T(8,128)(2,1)} fusion(bf16[256,1664]{1,0:T(8,128)(2,1)S(1)} %copy-done, bf16[4096,1664]{1,0:T(8,128)(2,1)} %all-gather.2.cloned.1.call-done, bf16[1664,256]{1,0:T(8,128)(2,1)S(1)} %copy-done.14, f32[256]{0:T(256)S(1)} %copy-done.15), kind=kOutput, calls=%fused_computation.3 | convolution fusion | flops 7055343616 | bytes 28967936 | tf_op jit(solution)/shard_map/dot_general | solution.py:86
  142.6 0.0 reduce-scatter.2.cloned.1.call-update
  142.6 0.6 copy-done.13
  143.2 0.1 fusion.80
  143.3 0.1 reduce_window_sum.11
  143.4 0.2 select_reduce_fusion
  143.6 105.9 %reduce-scatter.2.cloned.1.call-done = bf16[128,1664]{1,0:T(8,128)(2,1)} async-done(((bf16[4096,1664]{1,0:T(8,128)(2,1)}), bf16[128,1664]{1,0:T(8,128)(2,1)}) %reduce-scatter.2.cloned.1.call-update) | async-done | bytes 426000 | tf_op jit(solution)/shard_map/reduce_scatter | solution.py:85
  249.4 1.1 convert_add_fusion
  250.6 0.2 reshape.147
  250.8 0.5 reduce_sum.87
  251.3 0.1 fusion.53
  251.5 0.2 multiply_reduce_fusion.1
  251.7 3.8 %convolution_convert_fusion.1 = bf16[4,32,1664]{2,1,0:T(8,128)(2,1)S(1)} fusion(bf16[1664,1664]{1,0:T(8,128)(2,1)} %param.34, f32[32,1664]{1,0:T(8,128)S(1)} %reduce_sum.87, f32[1664]{0:T(1024)S(1)} %copy-done.11, f32[1664]{0:T(1024)S(1)} %copy-done.12, f32[32]{0:T(128)S(1)} %add_rsqrt_fusion, f32[32]{0:T(128)S(1)} %broadcast_multiply_fusion, ...), kind=kOutput, calls=%fused_computation.27 | convolution fusion | flops 191483904 | bytes 6198144 | tf_op jit(solution)/shard_map/osm,md->osd/dot_general | solution.py:105
  255.5 11.6 %all_to_all.5 = bf16[4,32,1664]{2,1,0:T(8,128)(2,1)S(1)} all-to-all(bf16[4,32,1664]{2,1,0:T(8,128)(2,1)S(1)} %convolution_convert_fusion.1), channel_id=1, replica_groups=mesh['blk'=32,'tok'=4] {'tok'}, dimensions={0} | all-to-all | bytes 851968 | tf_op jit(solution)/shard_map/all_to_all | solution.py:108
  267.1 0.8 copy.40
  (41 shorter events, 0.1 us)
Async XLA Ops:
  7.2 107.6 %copy-start = (bf16[256,1664]{1,0:T(8,128)(2,1)S(1)}, bf16[256,1664]{1,0:T(8,128)(2,1)}, u32[]{:S(2)}) copy-start(bf16[256,1664]{1,0:T(8,128)(2,1)} %param.31) | copy-start | bytes 2555908
  7.2 16.6 %copy-start.7 = (bf16[128,1664]{1,0:T(8,128)(2,1)S(1)}, bf16[128,1664]{1,0:T(8,128)(2,1)}, u32[]{:S(2)}) copy-start(bf16[128,1664]{1,0:T(8,128)(2,1)} %param.19) | copy-start | bytes 1277956
  7.2 6.4 %copy-start.3 = (bf16[128,1664]{1,0:T(8,128)(2,1)S(1)}, bf16[128,1664]{1,0:T(8,128)(2,1)}, u32[]{:S(2)}) copy-start(bf16[128,1664]{1,0:T(8,128)(2,1)} %param.20) | copy-start | bytes 1277956
  7.2 10.0 %copy-start.5 = (bf16[128,1664]{1,0:T(8,128)(2,1)S(1)}, bf16[128,1664]{1,0:T(8,128)(2,1)}, u32[]{:S(2)}) copy-start(bf16[128,1664]{1,0:T(8,128)(2,1)} %param.21) | copy-start | bytes 1277956
  7.2 107.5 %all-gather.2.cloned.1.call-start = ((), (), s32[]{:S(2)}) async-start(), calls=%async_computation.2 | async-start | bytes 14057472 | tf_op jit(solution)/shard_map/all_gather | solution.py:78
  7.3 17.5 %copy-start.9 = (s32[4096]{0:T(1024)S(1)}, s32[4096]{0:T(1024)}, u32[]{:S(2)}) copy-start(s32[4096]{0:T(1024)} %param.22) | copy-start | bytes 49156
  14.5 15.2 %copy-start.2 = (bf16[128,1664]{1,0:T(8,128)(2,1)}, bf16[128,1664]{1,0:T(8,128)(2,1)S(1)}, u32[]{:S(2)}) copy-start(bf16[128,1664]{1,0:T(8,128)(2,1)S(1)} %scatter_fusion) | copy-start | bytes 1277956
  14.5 10.5 %collective-permute-start.2 = (bf16[128,1664]{1,0:T(8,128)(2,1)S(1)}, bf16[128,1664]{1,0:T(8,128)(2,1)S(1)}, u32[]{:S(2)}, u32[]{:S(2)}) collective-permute-start(bf16[128,1664]{1,0:T(8,128)(2,1)S(1)} %scatter_fusion), channel_id=1, source_target_pairs={{0,4},{4,8},{8,12},{12,16},{16,20},{20,24},{24,28},{28,32},{32,36}... | collective-permute-start | bytes 1277960 | tf_op jit(solution)/shard_map/ppermute | solution.py:12
  15.9 9.9 %collective-permute-start.3 = (bf16[128,1664]{1,0:T(8,128)(2,1)S(1)}, bf16[128,1664]{1,0:T(8,128)(2,1)}, u32[]{:S(2)}, u32[]{:S(2)}) collective-permute-start(bf16[128,1664]{1,0:T(8,128)(2,1)S(1)} %scatter_fusion), channel_id=1, source_target_pairs={{4,0},{8,4},{12,8},{16,12},{20,16},{24,20},{28,24},{32,28},{36,32}... | collective-permute-start | bytes 1277960 | tf_op jit(solution)/shard_map/ppermute | solution.py:12
  17.2 11.4 %collective-permute-start = (bf16[128,1664]{1,0:T(8,128)(2,1)S(1)}, bf16[128,1664]{1,0:T(8,128)(2,1)S(1)}, u32[]{:S(2)}, u32[]{:S(2)}) collective-permute-start(bf16[128,1664]{1,0:T(8,128)(2,1)S(1)} %copy-done.5), channel_id=1, source_target_pairs={{0,4},{4,8},{8,12},{12,16},{16,20},{20,24},{24,28},{28,32},{32,36}... | collective-permute-start | bytes 1277960 | tf_op jit(solution)/shard_map/ppermute | solution.py:12
  22.4 6.1 %collective-permute-start.1 = (bf16[128,1664]{1,0:T(8,128)(2,1)S(1)}, bf16[128,1664]{1,0:T(8,128)(2,1)}, u32[]{:S(2)}, u32[]{:S(2)}) collective-permute-start(bf16[128,1664]{1,0:T(8,128)(2,1)S(1)} %copy-done.5), channel_id=1, source_target_pairs={{4,0},{8,4},{12,8},{16,12},{20,16},{24,20},{28,24},{32,28},{36,32}... | collective-permute-start | bytes 1277960 | tf_op jit(solution)/shard_map/ppermute | solution.py:12
  25.0 0.8 copy-start.6
  31.3 4.4 %copy-start.4 = (bf16[384,1664]{0,1:T(8,128)(2,1)S(1)}, bf16[384,1664]{0,1:T(8,128)(2,1)}, u32[]{:S(2)}) copy-start(bf16[384,1664]{0,1:T(8,128)(2,1)} %copy.30) | copy-start | bytes 3833860
  35.7 2.9 %copy-start.1 = (bf16[128,1664]{1,0:T(8,128)(2,1)S(1)}, bf16[128,1664]{1,0:T(8,128)(2,1)}, u32[]{:S(2)}) copy-start(bf16[128,1664]{1,0:T(8,128)(2,1)} %param.18) | copy-start | bytes 1277956
  38.2 0.8 copy-start.10
  38.2 76.5 %copy-start.15 = (f32[256]{0:T(256)S(1)}, f32[256]{0:T(256)}, u32[]{:S(2)}) copy-start(f32[256]{0:T(256)} %param.30) | copy-start | bytes 3076
  38.5 76.2 %copy-start.14 = (bf16[1664,256]{1,0:T(8,128)(2,1)S(1)}, bf16[1664,256]{1,0:T(8,128)(2,1)}, u32[]{:S(2)}) copy-start(bf16[1664,256]{1,0:T(8,128)(2,1)} %param.29) | copy-start | bytes 2555908
  40.0 209.4 %reduce-scatter.2.cloned.1.call-start = ((), (), s32[]{:S(2)}) async-start(), calls=%async_computation.3 | async-start | bytes 14057472 | tf_op jit(solution)/shard_map/reduce_scatter | solution.py:85
  142.6 0.7 copy-start.13
  143.2 108.1 %copy-start.8 = (f32[1664]{0:T(1024)S(1)}, f32[1664]{0:T(1024)}, u32[]{:S(2)}) copy-start(f32[1664]{0:T(1024)} %param.32) | copy-start | bytes 19972
  143.2 108.5 %copy-start.11 = (f32[1664]{0:T(1024)S(1)}, f32[1664]{0:T(1024)}, u32[]{:S(2)}) copy-start(f32[1664]{0:T(1024)} %param.35) | copy-start | bytes 19972
  143.2 108.5 %copy-start.12 = (f32[1664]{0:T(1024)S(1)}, f32[1664]{0:T(1024)}, u32[]{:S(2)}) copy-start(f32[1664]{0:T(1024)} %param.33) | copy-start | bytes 19972
Sparse Core Ops, SparseCore 0:
  40.1 74.5 all-gather.1
  142.7 106.6 reduce-scatter.1
where the time goes:
time: 275 us
  waiting for transfers between devices  180 us (65%)
  matrix products  42 us (15%)
  between operations  14.3 us (5%)
  blocking collectives  11.6 us (4%)
  local copies, waits for them, and re-layouts  9.54 us (3%)
  starting transfers between devices  9.43 us (3%)
  other arithmetic  7.38 us (3%)
    reduce_scatter x1, waiting for transfers between devices, body(): lax.psum_scatter(jnp.dot(group_units, w_proj, preferred_element_type=jnp....  106 us
    all_gather x1, waiting for transfers between devices, body(): lax.all_gather(normed, 'blk', axis=0, tiled=True)  74.5 us
    dot_general x1, matrix products, body(): jnp.dot(group_units, w_proj, preferred_element_type=jnp.float32)  27.8 us
    all_to_all x1, blocking collectives, body(): lax.all_to_all(outgoing, 'tok', split_axis=0, concat_axis=0, tiled=True)  11.6 us
    ppermute x4, starting transfers between devices, passed_along(): return lax.ppermute(block, axis, route)  9.17 us
  transfers between devices with their start and end apart: 6, of which 2 were waited for; matrix products, arithmetic and copies ran while one was open for 2% of the time, Pallas kernels for 0%

commit v1 on v0

--- a/solution.py
+++ b/solution.py
@@ -4,6 +4,13 @@
 from jax.sharding import PartitionSpec as P
 
 HEADS = 16
+
+
+def swapped_in(x, name, along):
+    peers = lax.axis_size(name)
+    pieces = jnp.stack([x for _ in range(peers)])
+    pieces = lax.all_to_all(pieces, name, split_axis=0, concat_axis=0)
+    return jnp.concatenate(pieces, axis=along)
 
 
 def passed_along(block, axis, distance):
@@ -74,12 +81,7 @@
     mixed = stream.astype(jnp.float32) + attended.astype(jnp.float32)
     normed = layer_norm(mixed, mlp_gain).astype(jnp.bfloat16)
     group_units = jax.nn.gelu(
-        jnp.dot(
-            lax.all_gather(normed, "blk", axis=0, tiled=True),
-            w_fc,
-            preferred_element_type=jnp.float32,
-        )
-        + b_fc,
+        jnp.dot(swapped_in(normed, "blk", 0), w_fc, preferred_element_type=jnp.float32) + b_fc,
         approximate=False,
     ).astype(jnp.bfloat16)
     summed = lax.psum_scatter(

time: 275 us -> 372 us (1.35)
  blocking collectives: 11.6 us -> 179 us
  waiting for transfers between devices: 180 us -> 105 us
  local copies, waits for them, and re-layouts: 9.54 us -> 16.1 us
    all_to_all x0 -> x1, blocking collectives: none -> 167 us  [swapped_in(): pieces = lax.all_to_all(pieces, name, split_axis=0, concat_axis=0)]
    all_gather x1 -> x0, waiting for transfers between devices: 74.5 us -> none  [body(): lax.all_gather(normed, 'blk', axis=0, tiled=True)]
    another operation x0 -> x1, local copies, waits for them, and re-layouts: none -> 6.59 us  [swapped_in(): pieces = jnp.stack([x for _ in range(peers)])]
  transfers between devices with their start and end apart: 6 -> 5, of which waited for: 2 -> 1; matrix products, arithmetic and copies ran while one was open for 2% -> 1% of each run, Pallas kernels for 0% -> 0%
where the time goes in v1:
time: 372 us
  blocking collectives  179 us (48%)
  waiting for transfers between devices  105 us (28%)
  matrix products  42 us (11%)
  local copies, waits for them, and re-layouts  16.1 us (4%)
  between operations  14.3 us (4%)
  starting transfers between devices  9.21 us (2%)
  other arithmetic  6.62 us (2%)
    all_to_all x1, blocking collectives, swapped_in(): pieces = lax.all_to_all(pieces, name, split_axis=0, concat_axis=0)  167 us
    reduce_scatter x1, waiting for transfers between devices, body(): lax.psum_scatter(jnp.dot(group_units, w_proj, preferred_element_type=jnp....  105 us
    dot_general x1, matrix products, body(): jnp.dot(group_units, w_proj, preferred_element_type=jnp.float32)  27.8 us
    all_to_all x1, blocking collectives, body(): lax.all_to_all(outgoing, 'tok', split_axis=0, concat_axis=0, tiled=True)  11.6 us
    ppermute x4, starting transfers between devices, passed_along(): return lax.ppermute(block, axis, route)  9.17 us
  transfers between devices with their start and end apart: 5, of which 1 were waited for; matrix products, arithmetic and copies ran while one was open for 1% of the time, Pallas kernels for 0%

profile of v1, /device:TPU:0, one launch (start us, length us, event | category | flops | bytes accessed | tf_op | source)
XLA Modules:
  0.0 371.5 jit_solution(14682407387627105649)
XLA Ops:
  7.2 0.0 copy-start
  7.2 0.0 reduce-scatter.2.cloned.1.call-start
  7.3 0.8 compare_select_fusion
  8.1 1.7 gather_fusion
  9.8 0.1 convert_reduce_fusion
  9.9 0.2 fusion.58
  10.1 3.4 fusion.14
  13.6 0.9 scatter_fusion
  14.5 0.0 copy-start.3
  14.5 1.3 collective-permute-start.2
  15.9 1.3 collective-permute-start.3
  17.2 5.3 %collective-permute-start = (bf16[128,1664]{1,0:T(8,128)(2,1)S(1)}, bf16[128,1664]{1,0:T(8,128)(2,1)S(1)}, u32[]{:S(2)}, u32[]{:S(2)}) collective-permute-start(bf16[128,1664]{1,0:T(8,128)(2,1)S(1)} %copy-done.6), channel_id=1, source_target_pairs={{0,4},{4,8},{8,12},{12,16},{16,20},{20,24},{24,28},{28,32},{32,36}... | collective-permute-start | bytes 1277960 | tf_op jit(solution)/shard_map/ppermute | solution.py:19
  22.4 1.3 collective-permute-start.1
  23.8 1.0 copy.32
  24.7 0.1 dynamic_slice.6
  24.8 0.1 fusion.82
  24.9 0.1 broadcast_compare_fusion
  25.0 0.0 copy-start.7
  25.1 0.7 copy-done.7
  25.8 1.2 pad_maximum_fusion.1
  27.0 1.5 copy.31
  28.6 1.1 pad_maximum_fusion
  29.7 1.6 copy.30
  31.3 4.4 %fusion.118 = (f32[16,128]{1,0:T(8,128)S(1)}, f32[16,128,384]{1,2,0:T(8,128)}) fusion(pred[128,384]{0,1:T(8,128)(4,1)S(1)} %broadcast_compare_fusion, bf16[384,16,104]{0,2,1:T(8,128)(2,1)} %bitcast.35, bf16[128,16,104]{0,2,1:T(8,128)(2,1)} %bitcast.38), kind=kOutput, calls=%fused_computation.159 | convolution fusion | flops 166723968 | bytes 4907008 | tf_op jit(solution)/shard_map/sub | solution.py:77
  35.7 2.5 fusion.52
  38.2 0.0 copy-start.11
  38.2 0.3 copy.34
  38.5 0.2 fusion.73
  38.7 0.3 multiply_reduce_fusion
  39.0 0.2 multiply_convert_fusion
  39.2 6.6 %stack.2 = bf16[32,128,1664]{2,1,0:T(8,128)(2,1)} broadcast(bf16[128,1664]{1,0:T(8,128)(2,1)S(1)} %multiply_convert_fusion), dimensions={1,2} | broadcast | bytes 14057472 | tf_op jit(solution)/shard_map/stack | solution.py:11
  45.8 166.9 %all_to_all.10 = bf16[32,128,1664]{2,1,0:T(8,128)(2,1)} all-to-all(bf16[32,128,1664]{2,1,0:T(8,128)(2,1)} %stack.2), channel_id=1, replica_groups=mesh['blk'=32,'tok'=4] {'blk'}, dimensions={0} | all-to-all | bytes 27262976 | tf_op jit(solution)/shard_map/all_to_all | solution.py:12
  212.7 27.8 %convolution_convert_fusion = bf16[4096,1664]{1,0:T(8,128)(2,1)} fusion(bf16[256,1664]{1,0:T(8,128)(2,1)S(1)} %copy-done, bf16[4096,1664]{1,0:T(8,128)(2,1)} %bitcast.33, bf16[1664,256]{1,0:T(8,128)(2,1)S(1)} %copy-done.15, f32[256]{0:T(256)S(1)} %copy-done.16), kind=kOutput, calls=%fused_computation.3 | convolution fusion | flops 7055343616 | bytes 28967936 | tf_op jit(solution)/shard_map/dot_general | solution.py:88
  240.5 0.0 reduce-scatter.2.cloned.1.call-update
  240.5 0.6 copy-done.14
  241.1 0.1 fusion.80
  241.2 0.1 reduce_window_sum.11
  241.3 0.2 select_reduce_fusion
  241.5 104.7 %reduce-scatter.2.cloned.1.call-done = bf16[128,1664]{1,0:T(8,128)(2,1)} async-done(((bf16[4096,1664]{1,0:T(8,128)(2,1)}), bf16[128,1664]{1,0:T(8,128)(2,1)}) %reduce-scatter.2.cloned.1.call-update) | async-done | bytes 426000 | tf_op jit(solution)/shard_map/reduce_scatter | solution.py:87
  346.2 1.1 convert_add_fusion
  347.3 0.2 reshape.153
  347.6 0.0 copy-start.1
  347.6 0.5 reduce_sum.87
  348.1 0.1 fusion.53
  348.2 0.2 multiply_reduce_fusion.1
  348.5 3.8 %convolution_convert_fusion.1 = bf16[4,32,1664]{2,1,0:T(8,128)(2,1)S(1)} fusion(bf16[1664,1664]{1,0:T(8,128)(2,1)} %param.34, f32[32,1664]{1,0:T(8,128)S(1)} %reduce_sum.87, f32[1664]{0:T(1024)S(1)} %copy-done.12, f32[1664]{0:T(1024)S(1)} %copy-done.13, f32[32]{0:T(128)S(1)} %add_rsqrt_fusion, f32[32]{0:T(128)S(1)} %broadcast_multiply_fusion, ...), kind=kOutput, calls=%fused_computation.27 | convolution fusion | flops 191483904 | bytes 6198144 | tf_op jit(solution)/shard_map/osm,md->osd/dot_general | solution.py:107
  352.3 11.6 %all_to_all.11 = bf16[4,32,1664]{2,1,0:T(8,128)(2,1)S(1)} all-to-all(bf16[4,32,1664]{2,1,0:T(8,128)(2,1)S(1)} %convolution_convert_fusion.1), channel_id=1, replica_groups=mesh['blk'=32,'tok'=4] {'tok'}, dimensions={0} | all-to-all | bytes 851968 | tf_op jit(solution)/shard_map/all_to_all | solution.py:110
  363.9 0.8 copy.40
  (42 shorter events, 0.1 us)
Async XLA Ops:
  7.2 205.5 %copy-start = (bf16[256,1664]{1,0:T(8,128)(2,1)S(1)}, bf16[256,1664]{1,0:T(8,128)(2,1)}, u32[]{:S(2)}) copy-start(bf16[256,1664]{1,0:T(8,128)(2,1)} %param.31) | copy-start | bytes 2555908
  7.2 16.6 %copy-start.8 = (bf16[128,1664]{1,0:T(8,128)(2,1)S(1)}, bf16[128,1664]{1,0:T(8,128)(2,1)}, u32[]{:S(2)}) copy-start(bf16[128,1664]{1,0:T(8,128)(2,1)} %param.19) | copy-start | bytes 1277956
  7.2 6.4 %copy-start.4 = (bf16[128,1664]{1,0:T(8,128)(2,1)S(1)}, bf16[128,1664]{1,0:T(8,128)(2,1)}, u32[]{:S(2)}) copy-start(bf16[128,1664]{1,0:T(8,128)(2,1)} %param.20) | copy-start | bytes 1277956
  7.2 10.0 %copy-start.6 = (bf16[128,1664]{1,0:T(8,128)(2,1)S(1)}, bf16[128,1664]{1,0:T(8,128)(2,1)}, u32[]{:S(2)}) copy-start(bf16[128,1664]{1,0:T(8,128)(2,1)} %param.21) | copy-start | bytes 1277956
  7.2 339.0 %reduce-scatter.2.cloned.1.call-start = ((), (), s32[]{:S(2)}) async-start(), calls=%async_computation.3 | async-start | bytes 14057472 | tf_op jit(solution)/shard_map/reduce_scatter | solution.py:87
  7.3 17.5 %copy-start.10 = (s32[4096]{0:T(1024)S(1)}, s32[4096]{0:T(1024)}, u32[]{:S(2)}) copy-start(s32[4096]{0:T(1024)} %param.22) | copy-start | bytes 49156
  14.5 15.2 %copy-start.3 = (bf16[128,1664]{1,0:T(8,128)(2,1)}, bf16[128,1664]{1,0:T(8,128)(2,1)S(1)}, u32[]{:S(2)}) copy-start(bf16[128,1664]{1,0:T(8,128)(2,1)S(1)} %scatter_fusion) | copy-start | bytes 1277956
  14.5 10.5 %collective-permute-start.2 = (bf16[128,1664]{1,0:T(8,128)(2,1)S(1)}, bf16[128,1664]{1,0:T(8,128)(2,1)S(1)}, u32[]{:S(2)}, u32[]{:S(2)}) collective-permute-start(bf16[128,1664]{1,0:T(8,128)(2,1)S(1)} %scatter_fusion), channel_id=1, source_target_pairs={{0,4},{4,8},{8,12},{12,16},{16,20},{20,24},{24,28},{28,32},{32,36}... | collective-permute-start | bytes 1277960 | tf_op jit(solution)/shard_map/ppermute | solution.py:19
  15.9 9.9 %collective-permute-start.3 = (bf16[128,1664]{1,0:T(8,128)(2,1)S(1)}, bf16[128,1664]{1,0:T(8,128)(2,1)}, u32[]{:S(2)}, u32[]{:S(2)}) collective-permute-start(bf16[128,1664]{1,0:T(8,128)(2,1)S(1)} %scatter_fusion), channel_id=1, source_target_pairs={{4,0},{8,4},{12,8},{16,12},{20,16},{24,20},{28,24},{32,28},{36,32}... | collective-permute-start | bytes 1277960 | tf_op jit(solution)/shard_map/ppermute | solution.py:19
  17.2 11.4 %collective-permute-start = (bf16[128,1664]{1,0:T(8,128)(2,1)S(1)}, bf16[128,1664]{1,0:T(8,128)(2,1)S(1)}, u32[]{:S(2)}, u32[]{:S(2)}) collective-permute-start(bf16[128,1664]{1,0:T(8,128)(2,1)S(1)} %copy-done.6), channel_id=1, source_target_pairs={{0,4},{4,8},{8,12},{12,16},{16,20},{20,24},{24,28},{28,32},{32,36}... | collective-permute-start | bytes 1277960 | tf_op jit(solution)/shard_map/ppermute | solution.py:19
  22.4 6.1 %collective-permute-start.1 = (bf16[128,1664]{1,0:T(8,128)(2,1)S(1)}, bf16[128,1664]{1,0:T(8,128)(2,1)}, u32[]{:S(2)}, u32[]{:S(2)}) collective-permute-start(bf16[128,1664]{1,0:T(8,128)(2,1)S(1)} %copy-done.6), channel_id=1, source_target_pairs={{4,0},{8,4},{12,8},{16,12},{20,16},{24,20},{28,24},{32,28},{36,32}... | collective-permute-start | bytes 1277960 | tf_op jit(solution)/shard_map/ppermute | solution.py:19
  25.0 0.8 copy-start.7
  31.3 4.4 %copy-start.5 = (bf16[384,1664]{0,1:T(8,128)(2,1)S(1)}, bf16[384,1664]{0,1:T(8,128)(2,1)}, u32[]{:S(2)}) copy-start(bf16[384,1664]{0,1:T(8,128)(2,1)} %copy.30) | copy-start | bytes 3833860
  35.7 2.9 copy-start.2
  38.2 0.8 copy-start.11
  45.8 166.9 %copy-start.15 = (bf16[1664,256]{1,0:T(8,128)(2,1)S(1)}, bf16[1664,256]{1,0:T(8,128)(2,1)}, u32[]{:S(2)}) copy-start(bf16[1664,256]{1,0:T(8,128)(2,1)} %param.29) | copy-start | bytes 2555908
  45.8 166.9 %copy-start.16 = (f32[256]{0:T(256)S(1)}, f32[256]{0:T(256)}, u32[]{:S(2)}) copy-start(f32[256]{0:T(256)} %param.30) | copy-start | bytes 3076
  240.5 0.7 copy-start.14
  241.1 106.9 %copy-start.9 = (f32[1664]{0:T(1024)S(1)}, f32[1664]{0:T(1024)}, u32[]{:S(2)}) copy-start(f32[1664]{0:T(1024)} %param.32) | copy-start | bytes 19972
  241.1 107.3 %copy-start.12 = (f32[1664]{0:T(1024)S(1)}, f32[1664]{0:T(1024)}, u32[]{:S(2)}) copy-start(f32[1664]{0:T(1024)} %param.35) | copy-start | bytes 19972
  241.1 107.3 %copy-start.13 = (f32[1664]{0:T(1024)S(1)}, f32[1664]{0:T(1024)}, u32[]{:S(2)}) copy-start(f32[1664]{0:T(1024)} %param.33) | copy-start | bytes 19972
  347.6 17.1 %copy-start.1 = (bf16[256,1664]{1,0:T(8,128)(2,1)S(1)}, bf16[256,1664]{1,0:T(8,128)(2,1)}, u32[]{:S(2)}) copy-start(bf16[256,1664]{1,0:T(8,128)(2,1)} %param.31) | copy-start | bytes 2555908
Sparse Core Ops, SparseCore 0:
  240.6 105.4 reduce-scatter.1
